TPU v7x, 32 devices: a whole 2x2x4 slice. The times are simulated.
32 devices in a mesh: seq: 32 (over z, y, x, core), chan: 1.
Axes of the slice: x: 2, y: 2, z: 4, core: 2. Of those that a mesh axis runs over, the one named last changes fastest.
Arguments:
- proj_in: bfloat16 [5120, 3, 8192], P('seq', None, 'chan'), may hold values from -6 to 6
- short_taps: float32 [7, 3, 8192], P(None, None, 'chan'), may hold values from -2.4 to 2.4
- long_taps: float32 [128, 8192], P(None, 'chan'), may hold values from -0.5 to 0.5
- skip_gain: float32 [8192], P('chan'), may hold values from -1 to 1
- keep: int32 [8192], P('chan'), may hold values from 0 to 1, as said below
- w_out: bfloat16 [8192, 4096], P('chan', 'seq'), may hold values from -0.09375 to 0.09375
- grad_out: bfloat16 [5120, 4096], P('seq', 'chan'), may hold values from -6 to 6
Outputs:
- output: bfloat16 [5120, 4096], P('seq', 'chan')
- grad_proj_in: bfloat16 [5120, 3, 8192], P('seq', None, 'chan')
- grad_long_taps: float32 [128, 8192], P(None, 'chan')
- grad_short_taps: float32 [7, 3, 8192], P(None, None, 'chan')
- grad_skip_gain: float32 [8192], P('chan')
Inputs may be any that keep to these rules, and one draw needn't show every extreme that they name: `keep`: in every aligned group of 16 consecutive channels exactly half of the entries are 1 and the rest 0.
All inputs are finite; a program needn't handle non-finite values.
Results may differ from a plain program's by a relative error of at most 0.012.
Values may be sent and summed in bfloat16 or wider, within the bound.
A program may use at most 192 MiB of HBM per device.

v0:
```python
import jax
import jax.numpy as jnp
from jax import lax
from jax.sharding import PartitionSpec as P


def shifted(x, axis, by):
    peers = lax.axis_size(axis)
    pairs = [(i, i + by) for i in range(peers) if 0 <= i + by < peers]
    return lax.ppermute(x, axis, pairs)


def depthwise(signal, kernel):
    result = lax.conv_general_dilated(
        signal[None],
        kernel[:, None, :],
        (1,),
        "VALID",
        dimension_numbers=("NWC", "WIO", "NWC"),
        feature_group_count=signal.shape[1],
        precision=lax.Precision.HIGHEST,
    )
    return result[0]


def local(proj_in, short_taps, long_taps, skip_gain, keep, w_out, grad_out):
    tokens = proj_in.shape[0]
    channels = proj_in.shape[2]
    tap_count = long_taps.shape[0]
    short_len = short_taps.shape[0]
    flat_width = 3 * channels
    short_flip = short_taps[::-1].reshape(short_len, flat_width)
    before = shifted(proj_in[tokens - short_len + 1 :], "seq", 1)
    padded_in = (
        jnp.concatenate([before, proj_in], axis=0)
        .reshape(tokens + short_len - 1, flat_width)
        .astype(jnp.float32)
    )
    short_mixed = depthwise(padded_in, short_flip).reshape(tokens, 3, channels)
    key_value = (short_mixed[:, 1] * short_mixed[:, 2]).astype(jnp.bfloat16)
    kv_before = shifted(key_value[tokens - tap_count + 1 :], "seq", 1)
    padded_kv = jnp.concatenate([kv_before, key_value], axis=0).astype(jnp.float32)
    key_value_f = key_value.astype(jnp.float32)
    queries = short_mixed[:, 0]
    filtered = depthwise(padded_kv, long_taps[::-1]) + skip_gain * key_value_f
    keep_f = keep.astype(jnp.float32)
    gated_out = (queries * filtered * keep_f).astype(jnp.bfloat16)
    live_rank = jnp.cumsum(keep) - 1
    slot_ids = lax.broadcasted_iota(jnp.int32, (channels, channels // 2), 1)
    packed = jnp.where((live_rank[:, None] == slot_ids) & (keep[:, None] == 1), 1.0, 0.0).astype(
        jnp.bfloat16
    )
    inputs = jnp.dot(gated_out, packed, preferred_element_type=jnp.float32).astype(jnp.bfloat16)
    local_rows = jnp.dot(packed.T, w_out, preferred_element_type=jnp.float32).astype(jnp.bfloat16)
    weight_panel = lax.all_gather(local_rows, "seq", axis=1, tiled=True)
    summed = lax.psum_scatter(
        lax.dot_general(
            weight_panel, inputs, (((0,), (1,)), ((), ())), preferred_element_type=jnp.float32
        ).astype(jnp.bfloat16),
        "chan",
        scatter_dimension=0,
        tiled=True,
    ).astype(jnp.float32)
    output = summed.T.astype(jnp.bfloat16)
    grad_inputs = lax.dot_general(
        lax.all_gather(grad_out, "chan", axis=1, tiled=True),
        weight_panel,
        (((1,), (1,)), ((), ())),
        preferred_element_type=jnp.float32,
    )
    slot_of = jnp.clip(live_rank, 0, channels // 2 - 1)
    grad_gated = jnp.take(grad_inputs, slot_of, axis=1) * keep_f
    grad_query = grad_gated * filtered
    grad_filtered = (grad_gated * queries).astype(jnp.bfloat16)
    following = shifted(grad_filtered[: tap_count - 1], "seq", -1)
    padded_grad = jnp.concatenate([grad_filtered, following], axis=0).astype(jnp.float32)
    grad_filt_f = grad_filtered.astype(jnp.float32)
    grad_key_value = depthwise(padded_grad, long_taps) + skip_gain * grad_filt_f
    grad_long = depthwise(padded_kv, grad_filt_f)[::-1]
    grad_gain = jnp.sum(grad_filt_f * key_value_f, axis=0)
    grad_mixed = jnp.stack(
        [grad_query, grad_key_value * short_mixed[:, 2], grad_key_value * short_mixed[:, 1]], axis=1
    ).astype(jnp.bfloat16)
    next_rows = shifted(grad_mixed[: short_len - 1], "seq", -1)
    padded_mixed = (
        jnp.concatenate([grad_mixed, next_rows], axis=0)
        .reshape(tokens + short_len - 1, flat_width)
        .astype(jnp.float32)
    )
    grad_proj_in = (
        depthwise(padded_mixed, short_taps.reshape(short_len, flat_width))
        .reshape(tokens, 3, channels)
        .astype(jnp.bfloat16)
    )
    grad_short = depthwise(padded_in, grad_mixed.reshape(tokens, flat_width).astype(jnp.float32))[
        ::-1
    ].reshape(short_len, 3, channels)
    reduced = lax.psum((grad_long, grad_short, grad_gain), "seq")
    return (output, grad_proj_in, reduced[0], reduced[1], reduced[2])


def solution(mesh):
    placed = (
        P("seq", None, "chan"),
        P(None, None, "chan"),
        P(None, "chan"),
        P("chan"),
        P("chan"),
        P("chan", "seq"),
        P("seq", "chan"),
    )
    return jax.shard_map(
        local,
        mesh=mesh,
        in_specs=placed,
        out_specs=(
            P("seq", "chan"),
            P("seq", None, "chan"),
            P(None, "chan"),
            P(None, None, "chan"),
            P("chan"),
        ),
        check_vma=False,
    )
```

profile of v0, /device:TPU:0, one launch (start us, length us, event | category | flops | bytes accessed | tf_op | source)
XLA Modules:
  0.0 1015.8 jit_solution(16170173250192499257)
XLA Ops:
  10.8 47.3 %fusion.49 = bf16[4096,128]{1,0:T(8,128)(2,1)} fusion(bf16[8192,128]{1,0:T(8,128)(2,1)S(1)} %copy-done, s32[8192]{0:T(1024)S(1)} %get-tuple-element.16, pred[8192]{0:T(1024)(128)(4,1)S(1)} %broadcast_compare_fusion), kind=kOutput, calls=%fused_computation.64 | convolution fusion | flops 8724676608 | bytes 3186688 | tf_op jit(solution)/shard_map/dot_general | solution.py:54
  64.0 32.7 %rev.13 = f32[128,8192]{1,0:T(8,128)} reverse(f32[128,8192]{1,0:T(8,128)} %param.9), dimensions={0} | reverse | bytes 8388608 | tf_op jit(solution)/shard_map/rev | solution.py:45
  96.7 8.9 pad_maximum_fusion.1
  105.6 10.1 copy.20
  115.8 20.0 %broadcast_in_dim.50 = bf16[1,166,24576]{2,1,0:T(8,128)(2,1)} reshape(bf16[166,3,8192]{2,1,0:T(4,128)(2,1)} %copy.20) | data formatting | bytes 16318464 | tf_op jit(solution)/shard_map/broadcast_in_dim | solution.py:15
  135.8 8.0 pad
  143.8 10.0 reshape.195
  153.8 11.7 %copy.22 = bf16[1,8,21,24576]{3,1,2,0:T(8,128)(2,1)} copy(bf16[1,8,21,24576]{3,2,1,0:T(8,128)(2,1)} %reshape.195) | data formatting | bytes 16515072 | tf_op jit(solution)/shard_map/conv_general_dilated | solution.py:14
  167.7 10.1 convolution_select_fusion.1
  177.8 13.4 %copy.24 = f32[8,21,24576]{2,1,0:T(8,128)} copy(f32[8,21,24576]{2,0,1:T(8,128)S(1)} %convolution_select_fusion.1) | data formatting | bytes 33030144 | tf_op jit(solution)/shard_map/conv_general_dilated | solution.py:14
  191.2 15.1 %reshape.199 = f32[1,168,24576]{2,1,0:T(8,128)} reshape(f32[8,21,24576]{2,1,0:T(8,128)} %copy.24) | data formatting | bytes 33030144 | tf_op jit(solution)/shard_map/conv_general_dilated | solution.py:14
  206.4 13.0 %slice.50 = f32[1,160,24576]{2,1,0:T(8,128)} slice(f32[1,168,24576]{2,1,0:T(8,128)} %reshape.199), slice={[0:1], [0:160], [0:24576]} | slice | bytes 31457280 | tf_op jit(solution)/shard_map/conv_general_dilated | solution.py:14
  219.3 23.2 %reshape_squeeze.4 = f32[160,3,8192]{2,1,0:T(4,128)} reshape(f32[1,160,24576]{2,1,0:T(8,128)} %slice.50) | data formatting | bytes 31457280 | tf_op jit(solution)/shard_map/reshape;squeeze | solution.py:39
  242.6 33.8 %multiply_convert_fusion = (bf16[160,1,8192]{2,1,0:T(2,128)(2,1)}, f32[160,1,8192]{2,1,0:T(1,128)}) fusion(f32[160,3,8192]{2,1,0:T(4,128)} %reshape_squeeze.4), kind=kLoop, calls=%fused_computation.60 | loop fusion | flops 2621440 | bytes 23592960 | tf_op jit(solution)/shard_map/convert_element_type | solution.py:40
  276.4 6.5 slice.54
  285.1 5.7 collective-permute-start.1
  290.8 18.7 %convolution_bitcast_fusion.1 = f32[160,4096]{1,0:T(8,128)} fusion(bf16[4096,4096]{1,0:T(8,128)(2,1)} %all-gather.2.cloned.1.call-done, bf16[160,4096]{1,0:T(8,128)(2,1)} %param.13), kind=kOutput, calls=%fused_computation.61 | convolution fusion | flops 5368709120 | bytes 37486592 | tf_op jit(solution)/shard_map/dot_general | solution.py:65
  309.4 4.9 copy.28
  314.3 33.7 %gather_fusion = f32[8192,160]{1,0:T(8,128)} fusion(f32[160,4096]{0,1:T(8,128)} %copy.28, s32[8192]{0:T(1024)S(1)} %broadcast_clamp_fusion), kind=kCustom, calls=%fused_computation | custom fusion | bytes 10518528 | tf_op jit(solution)/shard_map/jit(_take)/gather | solution.py:72
  347.9 8.4 copy.29
  356.4 14.0 %fusion.42 = (f32[8192]{0:T(1024)}, bf16[160,8192]{1,0:T(8,128)(2,1)S(1)}, bf16[160,8192]{1,0:T(8,128)(2,1)}) fusion(f32[160,1,8192]{2,1,0:T(1,128)} %get-tuple-element.20, f32[8192]{0:T(1024)S(1)} %copy-done.15, f32[8192,160]{0,1:T(8,128)} %copy.29, pred[8192]{0:T(1024)(128)(4,1)S(1)} %copy-done.19, bf16[160,1,8192]{2,1,0:T(2,128)(2,1)} %get-tuple-element.19), kind=kLoop, calls=%fused_computation.50 | loop fusion | flops 10477568 | bytes 18423808 | tf_op jit(solution)/shard_map/reduce_sum | solution.py:80
  373.5 3.0 fusion.44
  376.5 5.5 maximum_bitcast_fusion
  382.1 73.9 %fusion.32 = f32[1,128,8192]{2,0,1:T(1,128)} fusion(bf16[1,287,8192]{2,1,0:T(8,128)(2,1)} %maximum_bitcast_fusion, f32[160,1,8192]{2,0,1:T(8,128)} %fusion.44, f32[160,3,8192]{2,1,0:T(4,128)S(1)} %bitcast.80), kind=kOutput, calls=%fused_computation.38 | convolution fusion | flops 338165760 | bytes 19382272 | tf_op jit(solution)/shard_map/conv_general_dilated | solution.py:14
  456.0 63.8 %fusion.45 = (bf16[160,1,8192]{2,1,0:T(2,128)(2,1)}, f32[1,160,8192]{2,0,1:T(1,128)S(1)}) fusion(bf16[160,1,8192]{2,1,0:T(2,128)(2,1)S(1)} %copy-done.3, f32[160,1,8192]{2,0,1:T(8,128)S(1)} %copy-done.7, f32[8192]{0:T(1024)S(1)} %copy-done.20, f32[128,1,8192]{2,0,1:T(8,128)S(1)} %bitcast.87, bf16[1,287,8192]{2,1,0:T(8,128)(2,1)S(1)} %copy-done.9), kind=kOutput, calls=%fused_computation.56 | convolution fusion | flops 2019819520 | bytes 24657920 | tf_op jit(solution)/shard_map/conv_general_dilated | solution.py:14
  523.2 42.8 %fusion.48.clone.4 = bf16[160,4096]{1,0:T(8,128)(2,1)S(1)} fusion(s32[8192]{0:T(1024)S(1)} %copy-done.22, pred[8192]{0:T(1024)(128)(4,1)S(1)} %copy-done.24, f32[160,8192]{1,0:T(8,128)S(1)} %mul.84, f32[160,8192]{1,0:T(8,128)S(1)} %mul.81, bf16[160,8192]{1,0:T(8,128)(2,1)S(1)} %copy-done.6, f32[1,160,8192]{2,0,1:T(1,128)S(1)} %get-tuple-element.22, ...), kind=kOutput, calls=%fused_computation.63.clone.clone.clone.1 | convolution fusion | flops 10880155648 | bytes 24944640 | tf_op jit(solution)/shard_map/dot_general | solution.py:53
  566.0 5.3 copy.104
  571.3 32.9 %rev.14 = f32[128,8192]{1,0:T(8,128)} reverse(f32[128,8192]{1,0:T(8,128)} %bitcast.83), dimensions={0} | reverse | bytes 8388608 | tf_op jit(solution)/shard_map/rev | solution.py:79
  604.2 42.3 %psum.23 = f32[8192]{0:T(1024)} all-reduce(f32[8192]{0:T(1024)S(1)} %copy-done.18), channel_id=1, replica_groups=mesh['seq'=32,'chan'=1] {'seq'}, use_global_device_ids=true, to_apply=%region_5.6 | all-reduce | flops 8192 | bytes 65536 | tf_op jit(solution)/shard_map/psum | solution.py:98
  646.5 14.8 %convolution_convert_fusion = bf16[160,4096]{1,0:T(8,128)(2,1)} fusion(bf16[4096,4096]{1,0:T(8,128)(2,1)} %all-gather.2.cloned.1.call-done, bf16[160,4096]{1,0:T(8,128)(2,1)S(1)} %fusion.48.clone.4), kind=kOutput, calls=%fused_computation.62 | convolution fusion | flops 5369364480 | bytes 36175872 | tf_op jit(solution)/shard_map/dot_general | solution.py:57
  664.1 72.4 %slice_multiply_fusion = (bf16[160,1,8192]{2,1,0:T(2,128)(2,1)S(1)}, bf16[160,1,8192]{2,1,0:T(2,128)(2,1)S(1)}) fusion(f32[160,3,8192]{2,1,0:T(4,128)} %reshape_squeeze.4, f32[160,1,8192]{2,0,1:T(8,128)S(1)} %bitcast.85, f32[8192]{0:T(1024)S(1)} %copy-done.20, f32[128,1,8192]{2,0,1:T(8,128)S(1)} %bitcast.86, bf16[1,287,8192]{2,1,0:T(8,128)(2,1)S(1)} %maximum_bitcast_fusion.1), kind=kOutput, calls=%fused_computation.70 | convolution fusion | flops 2025062400 | bytes 35143680 | tf_op jit(solution)/shard_map/conv_general_dilated | solution.py:14
  736.5 18.8 %maximum_convert_fusion = bf16[160,3,8192]{2,1,0:T(4,128)(2,1)} fusion(bf16[160,1,8192]{2,1,0:T(2,128)(2,1)S(1)} %get-tuple-element.18, bf16[160,1,8192]{2,1,0:T(2,128)(2,1)S(1)} %get-tuple-element.17, bf16[160,1,8192]{2,1,0:T(2,128)(2,1)S(1)} %copy-done.8), kind=kLoop, calls=%fused_computation.20 | loop fusion | flops 23592960 | bytes 15728640 | tf_op jit(solution)/shard_map/convert_element_type | solution.py:83
  755.3 48.1 %convert_element_type.92 = bf16[160,1,24576]{2,1,0:T(2,128)(2,1)} reshape(bf16[160,3,8192]{2,1,0:T(4,128)(2,1)} %maximum_convert_fusion) | data formatting | bytes 15728640 | tf_op jit(solution)/shard_map/convert_element_type | solution.py:83
  806.6 40.4 %fusion.14 = f32[1,7,24576]{2,0,1:T(1,128)S(1)} fusion(bf16[160,1,24576]{2,1,0:T(2,128)(2,1)} %convert_element_type.92, bf16[1,166,24576]{2,1,0:T(8,128)(2,1)} %broadcast_in_dim.50), kind=kOutput, calls=%fused_computation.21 | convolution fusion | flops 55050240 | bytes 16711680 | tf_op jit(solution)/shard_map/conv_general_dilated | solution.py:14
  847.4 4.3 rev.15
  853.2 13.3 %pad_maximum_fusion = bf16[166,3,8192]{2,1,0:T(4,128)(2,1)} fusion(bf16[6,3,8192]{2,1,0:T(4,128)(2,1)} %collective-permute-done.3, bf16[160,3,8192]{2,1,0:T(4,128)(2,1)} %maximum_convert_fusion), kind=kLoop, calls=%fused_computation.23 | loop fusion | flops 4079616 | bytes 16318464 | tf_op jit(solution)/shard_map/concatenate | solution.py:86
  866.6 20.0 %broadcast_in_dim.61 = bf16[1,166,24576]{2,1,0:T(8,128)(2,1)} reshape(bf16[166,3,8192]{2,1,0:T(4,128)(2,1)} %pad_maximum_fusion) | data formatting | bytes 16318464 | tf_op jit(solution)/shard_map/broadcast_in_dim | solution.py:15
  886.6 7.6 pad.2
  894.2 10.3 %reshape.202 = bf16[1,8,21,24576]{3,2,1,0:T(8,128)(2,1)} reshape(bf16[1,168,24576]{2,1,0:T(8,128)(2,1)} %pad.2) | data formatting | bytes 16515072 | tf_op jit(solution)/shard_map/conv_general_dilated | solution.py:14
  904.5 11.8 %copy.35 = bf16[1,8,21,24576]{3,1,2,0:T(8,128)(2,1)} copy(bf16[1,8,21,24576]{3,2,1,0:T(8,128)(2,1)} %reshape.202) | data formatting | bytes 16515072 | tf_op jit(solution)/shard_map/conv_general_dilated | solution.py:14
  918.5 13.0 %fusion.11 = bf16[8,21,24576]{2,0,1:T(8,128)(2,1)} fusion(bf16[1,7,6,24576]{3,1,2,0:T(8,128)(2,1)S(1)} %slice.59, bf16[1,8,21,24576]{3,1,2,0:T(8,128)(2,1)} %copy.35, pred[8,21]{0,1:T(8,128)(4,1)S(1)} %copy-done.26, f32[7,1,24576]{2,0,1:T(8,128)S(1)} %bitcast.90), kind=kOutput, calls=%fused_computation.16 | convolution fusion | flops 386924544 | bytes 19267752 | tf_op jit(solution)/shard_map/conv_general_dilated | solution.py:14
  931.6 11.8 %copy.37 = bf16[8,21,24576]{2,1,0:T(8,128)(2,1)} copy(bf16[8,21,24576]{2,0,1:T(8,128)(2,1)} %fusion.11) | data formatting | bytes 16515072 | tf_op jit(solution)/shard_map/convert_element_type | solution.py:93
  943.3 10.0 reshape.206
  953.3 7.2 slice.60
  960.6 19.5 %convert_element_type.89 = bf16[160,3,8192]{2,1,0:T(4,128)(2,1)} reshape(bf16[1,160,24576]{2,1,0:T(8,128)(2,1)} %slice.60) | data formatting | bytes 15728640 | tf_op jit(solution)/shard_map/convert_element_type | solution.py:93
  980.1 13.1 %copy.41 = bf16[160,3,8192]{2,0,1:T(8,128)(2,1)} copy(bf16[160,3,8192]{2,1,0:T(4,128)(2,1)} %convert_element_type.89) | data formatting | bytes 15728640
  993.3 8.4 all-reduce.3.cloned.1.call-done
  1004.1 4.6 copy.109
  (110 shorter events, 33.0 us)
Async XLA Ops:
  7.2 3.6 copy-start
  7.2 283.6 %all-gather.2.cloned.1.call-start = ((), (), s32[]{:S(2)}) async-start(), calls=%async_computation | async-start | bytes 34603008 | tf_op jit(solution)/shard_map/all_gather | solution.py:55
  8.1 49.9 %copy-start.23 = (pred[8192]{0:T(1024)(128)(4,1)}, pred[8192]{0:T(1024)(128)(4,1)S(1)}, u32[]{:S(2)}) copy-start(pred[8192]{0:T(1024)(128)(4,1)S(1)} %broadcast_compare_fusion) | copy-start | bytes 24580
  10.2 0.6 copy-start.21
  10.8 51.0 %copy-start.17 = (s32[8192]{0:T(1024)S(1)}, s32[8192]{0:T(1024)}, u32[]{:S(2)}) copy-start(s32[8192]{0:T(1024)} %param.11) | copy-start | bytes 98308
  10.8 51.6 %copy-start.13 = (f32[7,3,8192]{2,0,1:T(8,128)S(1)}, f32[7,3,8192]{2,0,1:T(8,128)}, u32[]{:S(2)}) copy-start(f32[7,3,8192]{2,0,1:T(8,128)} %param.8) | copy-start | bytes 2064388
  58.1 943.6 %all-reduce.3.cloned.1.call-start = ((), (), s32[]{:S(2)}) async-start(), calls=%async_computation.1 | async-start | bytes 10223616 | tf_op jit(solution)/shard_map/psum | solution.py:98
  59.2 37.5 %collective-permute-start = (bf16[6,3,8192]{2,0,1:T(8,128)(2,1)S(1)}, bf16[6,3,8192]{2,0,1:T(8,128)(2,1)S(1)}, u32[]{:S(2)}, u32[]{:S(2)}) collective-permute-start(bf16[6,3,8192]{2,0,1:T(8,128)(2,1)S(1)} %slice.33), channel_id=1, source_target_pairs={{0,1},{1,2},{2,3},{3,4},{4,5},{5,6},{6,7},{7,8},{8,9},{9,10},{10,1... | collective-permute-start | bytes 884744 | tf_op jit(solution)/shard_map/ppermute | solution.py:10
  153.8 13.9 %copy-start.25 = (pred[8,21]{0,1:T(8,128)(4,1)S(1)}, pred[8,21]{0,1:T(8,128)(4,1)}, u32[]{:S(2)}) copy-start(pred[8,21]{0,1:T(8,128)(4,1)} %constant.50) | copy-start | bytes 508
  285.1 91.4 %collective-permute-start.1 = (bf16[127,8192]{1,0:T(8,128)(2,1)S(1)}, bf16[127,8192]{1,0:T(8,128)(2,1)}, u32[]{:S(2)}, u32[]{:S(2)}) collective-permute-start(bf16[127,8192]{1,0:T(8,128)(2,1)S(1)} %bitcast.89), channel_id=1, source_target_pairs={{0,1},{1,2},{2,3},{3,4},{4,5},{5,6},{6,7},{7,8},{8,9},{9,10},{10,1... | collective-permute-start | bytes 6242312 | tf_op jit(solution)/shard_map/ppermute | solution.py:10
  347.9 8.4 copy-start.15
  347.9 8.4 copy-start.19
  356.3 17.2 %copy-start.2 = (f32[8192,160]{0,1:T(8,128)S(1)}, f32[8192,160]{0,1:T(8,128)}, u32[]{:S(2)}) copy-start(f32[8192,160]{0,1:T(8,128)} %copy.29) | copy-start | bytes 15728644
  356.3 25.7 %slice-start = ((s8[20971520]{0:T(1024)(128)(4,1)}), s8[4194304]{0:T(1024)(128)(4,1)S(1)}, s32[]{:S(2)}) async-start(s8[20971520]{0:T(1024)(128)(4,1)} %bitcast.79), calls=%async_computation.2 | async-start | bytes 8388608
  356.3 25.6 %slice-start.1 = ((s8[20971520]{0:T(1024)(128)(4,1)}), s8[4194304]{0:T(1024)(128)(4,1)S(1)}, s32[]{:S(2)}) async-start(s8[20971520]{0:T(1024)(128)(4,1)} %bitcast.79), calls=%async_computation.3 | async-start | bytes 8388608
  356.4 25.6 %slice-start.2 = ((s8[20971520]{0:T(1024)(128)(4,1)}), s8[4194304]{0:T(1024)(128)(4,1)S(1)}, s32[]{:S(2)}) async-start(s8[20971520]{0:T(1024)(128)(4,1)} %bitcast.79), calls=%async_computation.4 | async-start | bytes 8388608
  370.3 6.1 copy-start.4
  371.9 10.1 slice-start.3
  371.9 289.4 %collective-permute-start.2 = (bf16[127,8192]{1,0:T(8,128)(2,1)}, bf16[127,8192]{1,0:T(8,128)(2,1)}, u32[]{:S(2)}, u32[]{:S(2)}) collective-permute-start(bf16[127,8192]{1,0:T(8,128)(2,1)} %slice.57), channel_id=1, source_target_pairs={{1,0},{2,1},{3,2},{4,3},{5,4},{6,5},{7,6},{8,7},{9,8},{10,9},{11,1... | collective-permute-start | bytes 6242312 | tf_op jit(solution)/shard_map/ppermute | solution.py:10
  376.5 5.5 slice-start.4
  382.0 73.9 %copy-start.3 = (bf16[160,1,8192]{2,1,0:T(2,128)(2,1)S(1)}, bf16[160,1,8192]{2,1,0:T(2,128)(2,1)}, u32[]{:S(2)}) copy-start(bf16[160,1,8192]{2,1,0:T(2,128)(2,1)} %get-tuple-element.19) | copy-start | bytes 7864324
  382.0 73.9 %copy-start.7 = (f32[160,1,8192]{2,0,1:T(8,128)S(1)}, f32[160,1,8192]{2,0,1:T(8,128)}, u32[]{:S(2)}) copy-start(f32[160,1,8192]{2,0,1:T(8,128)} %fusion.44) | copy-start | bytes 15728644
  382.0 73.9 %copy-start.9 = (bf16[1,287,8192]{2,1,0:T(8,128)(2,1)S(1)}, bf16[1,287,8192]{2,1,0:T(8,128)(2,1)}, u32[]{:S(2)}) copy-start(bf16[1,287,8192]{2,1,0:T(8,128)(2,1)} %maximum_bitcast_fusion) | copy-start | bytes 14106628
  382.1 73.9 %copy-start.11 = (f32[128,8192]{1,0:T(8,128)S(1)}, f32[128,8192]{1,0:T(8,128)}, u32[]{:S(2)}) copy-start(f32[128,8192]{1,0:T(8,128)} %rev.13) | copy-start | bytes 12582916
  382.1 73.9 %copy-start.20 = (f32[8192]{0:T(1024)S(1)}, f32[8192]{0:T(1024)}, u32[]{:S(2)}) copy-start(f32[8192]{0:T(1024)} %param.10) | copy-start | bytes 98308
  456.0 63.9 %copy-start.16 = (f32[8192]{0:T(1024)S(1)}, f32[8192]{0:T(1024)}, u32[]{:S(2)}) copy-start(f32[8192]{0:T(1024)} %convert_element_type.77) | copy-start | bytes 98308
  519.9 2.2 slice-start.5
  519.9 2.5 slice-start.6
  519.9 3.3 copy-start.6
  519.9 3.3 copy-start.22
  519.9 3.3 copy-start.24
  523.2 42.8 %copy-start.12 = (f32[1,128,8192]{2,0,1:T(1,128)S(1)}, f32[1,128,8192]{2,0,1:T(1,128)}, u32[]{:S(2)}) copy-start(f32[1,128,8192]{2,0,1:T(1,128)} %fusion.32) | copy-start | bytes 12582916
  571.3 32.9 %copy-start.18 = (f32[8192]{0:T(1024)S(1)}, f32[8192]{0:T(1024)}, u32[]{:S(2)}) copy-start(f32[8192]{0:T(1024)} %get-tuple-element.12) | copy-start | bytes 98308
  571.3 92.1 %slice-start.7 = ((s8[5242880]{0:T(1024)(128)(4,1)}), s8[1048576]{0:T(1024)(128)(4,1)S(1)}, s32[]{:S(2)}) async-start(s8[5242880]{0:T(1024)(128)(4,1)} %bitcast.84), calls=%async_computation.9 | async-start | bytes 2097152
  646.5 14.8 %copy-start.5 = (bf16[160,8192]{1,0:T(8,128)(2,1)S(1)}, bf16[160,8192]{1,0:T(8,128)(2,1)}, u32[]{:S(2)}) copy-start(bf16[160,8192]{1,0:T(8,128)(2,1)} %copy-done.4) | copy-start | bytes 7864324
  646.5 17.0 %slice-start.8 = ((s8[5242880]{0:T(1024)(128)(4,1)}), s8[4194304]{0:T(1024)(128)(4,1)S(1)}, s32[]{:S(2)}) async-start(s8[5242880]{0:T(1024)(128)(4,1)} %bitcast.84), calls=%async_computation.10 | async-start | bytes 8388608
  661.3 2.8 copy-start.10
  664.1 72.4 %copy-start.8 = (bf16[160,1,8192]{2,1,0:T(2,128)(2,1)S(1)}, bf16[160,1,8192]{2,1,0:T(2,128)(2,1)}, u32[]{:S(2)}) copy-start(bf16[160,1,8192]{2,1,0:T(2,128)(2,1)} %get-tuple-element.21) | copy-start | bytes 7864324
  805.3 47.9 %collective-permute-start.3 = (bf16[6,3,8192]{2,1,0:T(4,128)(2,1)}, bf16[6,3,8192]{2,1,0:T(4,128)(2,1)}, u32[]{:S(2)}, u32[]{:S(2)}) collective-permute-start(bf16[6,3,8192]{2,1,0:T(4,128)(2,1)} %slice.58), channel_id=1, source_target_pairs={{1,0},{2,1},{3,2},{4,3},{5,4},{6,5},{7,6},{8,7},{9,8},{10,9},{11,1... | collective-permute-start | bytes 884744 | tf_op jit(solution)/shard_map/ppermute | solution.py:10
  904.5 14.0 %copy-start.14 = (f32[7,3,8192]{2,0,1:T(8,128)S(1)}, f32[7,3,8192]{2,0,1:T(8,128)}, u32[]{:S(2)}) copy-start(f32[7,3,8192]{2,0,1:T(8,128)} %param.8) | copy-start | bytes 2064388
  904.5 14.0 %copy-start.26 = (pred[8,21]{0,1:T(8,128)(4,1)S(1)}, pred[8,21]{0,1:T(8,128)(4,1)}, u32[]{:S(2)}) copy-start(pred[8,21]{0,1:T(8,128)(4,1)} %constant.50) | copy-start | bytes 508
  980.1 28.6 %copy-start.1 = (bf16[8192,128]{1,0:T(8,128)(2,1)S(1)}, bf16[8192,128]{1,0:T(8,128)(2,1)}, u32[]{:S(2)}) copy-start(bf16[8192,128]{1,0:T(8,128)(2,1)} %param.12) | copy-start | bytes 6291460
Sparse Core Ops, SparseCore 0:
  58.2 195.3 all-gather.1
  853.4 148.2 all-reduce.2
where the time goes:
time: 1030 us; the launch traced here: 1020 us
  local copies, waits for them, and re-layouts  439 us (43%)
  matrix products  397 us (39%)
  other arithmetic  103 us (10%)
  blocking collectives  42.3 us (4%)
  between operations  14.8 us (1%)
  starting transfers between devices  11 us (1%)
    conv_general_dilated x6, matrix products, depthwise(): lax.conv_general_dilated(signal[None], kernel[:, None, :], (1,), 'VALID',...  274 us
    conv_general_dilated x9, local copies, waits for them, and re-layouts, depthwise(): lax.conv_general_dilated(signal[None], kernel[:, None, :], (1,), 'VALID',...  89.7 us
    broadcast_in_dim x4, local copies, waits for them, and re-layouts, depthwise(): signal[None]  55.6 us
    convert_element_type x4, local copies, waits for them, and re-layouts, local(): grad_proj_in = depthwise(padded_mixed, short_taps.reshape(short_len, flat...  48.5 us
    convert_element_type x1, local copies, waits for them, and re-layouts, local(): grad_mixed = jnp.stack([grad_query, grad_key_value * short_mixed[:, 2], g...  48.1 us
    dot_general x1, matrix products, local(): jnp.dot(packed.T, w_out, preferred_element_type=jnp.float32)  47.3 us
    dot_general x1, matrix products, local(): jnp.dot(gated_out, packed, preferred_element_type=jnp.float32)  42.8 us
    psum x1, blocking collectives, local(): reduced = lax.psum((grad_long, grad_short, grad_gain), 'seq')  42.3 us
  transfers between devices with their start and end apart: 6, of which 1 were waited for; matrix products, arithmetic and copies ran while one was open for 72% of the time, Pallas kernels for 0%

commit v1 on v0

v1 whole, which is shorter than its diff:
```python
import functools

import jax
import jax.numpy as jnp
import numpy as np
from jax import lax
from jax.experimental import pallas as pl
from jax.experimental.pallas import tpu as pltpu
from jax.sharding import PartitionSpec as P

GROUP = 16
EDGE = 8
CHUNKS = 4
F32 = jnp.float32
BF16 = jnp.bfloat16


def shifted(x, axis, by):
    peers = lax.axis_size(axis)
    pairs = [(i, i + by) for i in range(peers) if 0 <= i + by < peers]
    return lax.ppermute(x, axis, pairs)


def spectral(tokens, taps):
    length = tokens + taps
    freq = np.arange(length // 2) + 0.5
    angle = 2 * np.pi * freq[:, None] * np.arange(length)[None, :] / length
    return np.concatenate([np.cos(angle), -np.sin(angle)], axis=0)


def dot(a, b):
    return jnp.dot(a, b, preferred_element_type=F32)


def dot_nt(a, b):
    return lax.dot_general(a, b, (((1,), (1,)), ((), ())), preferred_element_type=F32)


def product(x, h, half):
    xr, xi, hr, hi = x[:half], x[half:], h[:half], h[half:]
    return jnp.concatenate([xr * hr - xi * hi, xr * hi + xi * hr], axis=0)


def product_conj(x, h, half):
    xr, xi, hr, hi = x[:half], x[half:], h[:half], h[half:]
    return jnp.concatenate([xr * hr + xi * hi, xi * hr - xr * hi], axis=0)


def selector(slot_row, wide):
    rows = lax.broadcasted_iota(jnp.int32, (wide // 2, wide), 0)
    return jnp.where(rows == slot_row, 1.0, 0.0).astype(BF16)


def pack_kernel(slot_ref, w_ref, out_ref):
    wide = w_ref.shape[0]
    out_ref[...] = dot(selector(slot_ref[0:1, :], wide), w_ref[...]).astype(BF16)


def mix_kernel(x_ref, edge_ref, short_ref, mixed_ref, kv_ref, pad):
    tokens = x_ref.shape[1]
    taps = short_ref.shape[1]
    for i in range(3):
        pad[0:EDGE, :] = edge_ref[i].astype(F32)
        pad[EDGE:, :] = x_ref[i].astype(F32)
        total = short_ref[i, 0:1, :] * pad[EDGE : EDGE + tokens, :]
        for j in range(1, taps):
            total += short_ref[i, j : j + 1, :] * pad[EDGE - j : EDGE - j + tokens, :]
        mixed_ref[i] = total
    kv_ref[...] = (mixed_ref[1] * mixed_ref[2]).astype(BF16)


def forward_kernel(
    own_ref, next_ref, inv_ref, kv_ref, before_ref, q_ref, long_ref, gain_ref, slot_ref,
    filtered_ref, gated_ref, kspec_ref, hspec_ref,
):
    half = own_ref.shape[0] // 2
    taps = long_ref.shape[0]
    wide = kv_ref.shape[1]
    kv = kv_ref[...]
    kspec = dot(own_ref[...], kv) - dot(next_ref[...], before_ref[...])
    hspec = dot(own_ref[:, :taps], long_ref[...].astype(BF16))
    spec = product(kspec, hspec, half)
    filtered = dot(inv_ref[...], spec.astype(BF16)) + gain_ref[0:1, :] * kv.astype(F32)
    filtered_ref[...] = filtered
    gated = (q_ref[0] * filtered).astype(BF16)
    gated_ref[...] = dot_nt(gated, selector(slot_ref[0:1, :], wide)).astype(BF16)
    kspec_ref[...] = kspec.astype(BF16)
    hspec_ref[...] = hspec.astype(BF16)


def grad_kernel(
    own_ref, inv_ref, panel_ref, go_ref, gated_ref, slot_ref, filtered_ref, q_ref, kv_ref, kspec_ref,
    out_ref, gq_ref, gf_ref, sums_ref,
):
    half = own_ref.shape[0] // 2
    taps = sums_ref.shape[0] - EDGE
    wide = kv_ref.shape[1]
    panel = panel_ref[...]

    @pl.when(pl.program_id(0) == 0)
    def _():
        out_ref[...] = jnp.zeros_like(out_ref)

    out_ref[...] += dot(gated_ref[...], panel)
    gi = dot_nt(go_ref[...], panel)
    gi_high = gi.astype(BF16)
    gi_low = (gi - gi_high.astype(F32)).astype(BF16)
    pick = selector(slot_ref[0:1, :], wide)
    gg = dot(gi_high, pick) + dot(gi_low, pick)
    gq_ref[...] = (gg * filtered_ref[...]).astype(BF16)
    gf = (gg * q_ref[0]).astype(BF16)
    gf_ref[...] = gf
    spec = product_conj(dot(own_ref[...], gf), kspec_ref[...].astype(F32), half)
    sums_ref[:taps, :] = dot(inv_ref[:taps, :], spec.astype(BF16))
    gain = jnp.sum(gf.astype(F32) * kv_ref[...].astype(F32), axis=0, keepdims=True)
    sums_ref[taps:, :] = jnp.broadcast_to(gain, (EDGE, wide))


def back_kernel(
    own_ref, next_ref, inv_ref, gf_ref, after_ref, hspec_ref, gain_ref, gq_ref, k_ref, v_ref, x_ref, edge_ref, short_ref,
    gp_ref, tail_ref, head_ref, gs_ref, pad, pad_x,
):
    half = own_ref.shape[0] // 2
    tokens = x_ref.shape[1]
    taps = short_ref.shape[1]
    gf = gf_ref[...]
    gspec = dot(own_ref[...], gf) + dot(next_ref[...], after_ref[...])
    spec = product_conj(gspec, hspec_ref[...].astype(F32), half)
    gkv = dot(inv_ref[...], spec.astype(BF16)) + gain_ref[0:1, :] * gf.astype(F32)
    grads = (
        gq_ref[...],
        (gkv * v_ref[0]).astype(BF16),
        (gkv * k_ref[0]).astype(BF16),
    )
    pad[tokens:, :] = jnp.zeros((EDGE, gf.shape[1]), F32)
    for i in range(3):
        gm = grads[i]
        tail_ref[i] = gm[tokens - 2 * EDGE :, :]
        head_ref[i] = gm[: 2 * EDGE, :]
        gmf = gm.astype(F32)
        pad[:tokens, :] = gmf
        pad_x[0:EDGE, :] = edge_ref[i].astype(F32)
        pad_x[EDGE:, :] = x_ref[i].astype(F32)
        total = short_ref[i, 0:1, :] * gmf
        gs_ref[i, 0:1, :] = jnp.sum(gmf * pad_x[EDGE:, :], axis=0, keepdims=True)
        for j in range(1, taps):
            total += short_ref[i, j : j + 1, :] * pad[j : j + tokens, :]
            gs_ref[i, j : j + 1, :] = jnp.sum(
                pad[:tokens, :] * pad_x[EDGE - j : EDGE - j + tokens, :], axis=0, keepdims=True
            )
        gs_ref[i, taps:, :] = jnp.zeros((EDGE - taps, gf.shape[1]), F32)
        gp_ref[i] = total.astype(BF16)


def tail_kernel(tail_ref, after_ref, short_ref, gp_ref, out_ref, pad):
    del gp_ref
    rows = tail_ref.shape[1]
    taps = short_ref.shape[1]
    for i in range(3):
        pad[:rows, :] = tail_ref[i].astype(F32)
        pad[rows:, :] = after_ref[i].astype(F32)
        total = short_ref[i, 0:1, :] * pad[:rows, :]
        for j in range(1, taps):
            total += short_ref[i, j : j + 1, :] * pad[j : j + rows, :]
        out_ref[i] = total.astype(BF16)


def params(flops=0, moved=0):
    return dict(
        compiler_params=pltpu.CompilerParams(
            dimension_semantics=("arbitrary",), vmem_limit_bytes=56 * 2**20
        ),
        cost_estimate=pl.CostEstimate(flops=flops, bytes_accessed=moved, transcendentals=0),
    )


def local(proj_in, short_taps, long_taps, skip_gain, keep, w_out, grad_out):
    tokens, _, channels = proj_in.shape
    tap_count = long_taps.shape[0]
    short_len = short_taps.shape[0]
    size = tokens + tap_count
    chunks = CHUNKS if channels % (CHUNKS * 512) == 0 else 1
    width = channels // chunks
    block = min(512, width)
    steps = width // block

    matrix = spectral(tokens, tap_count)
    own = jnp.asarray(matrix[:, :tokens], BF16)
    nxt = jnp.asarray(matrix[:, tokens:], BF16)
    inv = jnp.asarray(matrix[:, :tokens].T * (2.0 / size), BF16)

    x = proj_in.transpose(1, 0, 2)
    short = short_taps.transpose(1, 0, 2)
    gain = jnp.broadcast_to(skip_gain[None], (EDGE, channels))
    groups = keep.reshape(channels // GROUP, GROUP)
    rank = jnp.cumsum(groups, axis=1) - 1
    base = (jnp.arange(channels // GROUP, dtype=jnp.int32) % (block // GROUP)) * (GROUP // 2)
    slot = jnp.where(groups == 1, rank + base[:, None], -1).reshape(1, channels)
    slot = jnp.broadcast_to(slot, (EDGE, channels))
    go = lax.all_gather(grad_out, "chan", axis=1, tiled=True)
    features = w_out.shape[1]
    whole = pl.BlockSpec(memory_space=pltpu.VMEM)

    def two(rows, off=0, wide=block):
        return pl.BlockSpec((rows, wide), lambda c: (0, c + off))

    def three(lead, rows, off=0, at=0):
        return pl.BlockSpec((lead, rows, block), lambda c: (at, 0, c + off))

    def shape2(rows, kind, wide=width):
        return jax.ShapeDtypeStruct((rows, wide), kind)

    def shape3(lead, rows, kind):
        return jax.ShapeDtypeStruct((lead, rows, width), kind)

    panels = []
    for n in range(chunks):
        off = n * steps
        rows = pl.pallas_call(
            pack_kernel,
            grid=(steps,),
            in_specs=[two(EDGE, off), pl.BlockSpec((block, features), lambda c, off=off: (c + off, 0))],
            out_specs=pl.BlockSpec((block // 2, features), lambda c: (c, 0)),
            out_shape=jax.ShapeDtypeStruct((width // 2, features), BF16),
            name=f"pack{n}",
            **params(width * block * features, 3 * width * features),
        )(slot, w_out)
        panels.append(lax.all_gather(rows, "seq", axis=1, tiled=True))

    edge = shifted(x[:, tokens - EDGE :, :], "seq", 1)
    front = []
    for n in range(chunks):
        off = n * steps
        mixed, kv = pl.pallas_call(
            mix_kernel,
            grid=(steps,),
            in_specs=[three(3, tokens, off), three(3, EDGE, off), three(3, short_len, off)],
            out_specs=[three(3, tokens), two(tokens)],
            out_shape=[shape3(3, tokens, F32), shape2(tokens, BF16)],
            scratch_shapes=[pltpu.VMEM((tokens + EDGE, block), F32)],
            name=f"mix{n}",
            **params(42 * tokens * width, 20 * tokens * width),
        )(x, edge, short)
        before = shifted(kv[tokens - tap_count :], "seq", 1)
        front.append((mixed, kv, before))

    forward = []
    for n in range(chunks):
        off = n * steps
        mixed, kv, before = front[n]
        forward.append(
            pl.pallas_call(
                forward_kernel,
                grid=(steps,),
                in_specs=[
                    whole, whole, whole, two(tokens), two(tap_count), three(1, tokens),
                    two(tap_count, off), two(EDGE, off), two(EDGE, off),
                ],
                out_specs=[two(tokens), two(tokens, 0, block // 2), two(size), two(size)],
                out_shape=[
                    shape2(tokens, F32),
                    shape2(tokens, BF16, width // 2),
                    shape2(size, BF16),
                    shape2(size, BF16),
                ],
                name=f"forward{n}",
                **params(8 * size * tokens * width, 20 * tokens * width),
            )(own, nxt, inv, kv, before, mixed, long_taps, gain, slot)
        )

    totals, grads = None, []
    for n in range(chunks):
        off = n * steps
        mixed, kv, _ = front[n]
        filtered, gated, kspec, hspec = forward[n]
        out_wide = panels[n].shape[1]
        part, gq, gf, sums = pl.pallas_call(
            grad_kernel,
            grid=(steps,),
            in_specs=[
                whole, whole, pl.BlockSpec((block // 2, out_wide), lambda c: (c, 0)), whole,
                two(tokens, 0, block // 2), two(EDGE, off), two(tokens), three(1, tokens), two(tokens), two(size),
            ],
            out_specs=[pl.BlockSpec((tokens, out_wide), lambda c: (0, 0)), two(tokens), two(tokens), two(tap_count + EDGE)],
            out_shape=[
                jax.ShapeDtypeStruct((tokens, out_wide), F32),
                shape2(tokens, BF16), shape2(tokens, BF16), shape2(tap_count + EDGE, F32),
            ],
            name=f"grad{n}",
            **params(2 * tokens * width * out_wide, width * out_wide),
        )(own, inv, panels[n], go, gated, slot, filtered, mixed, kv, kspec)
        totals = part if totals is None else totals + part
        after = shifted(gf[:tap_count], "seq", -1)
        gp, tail, head, gs = pl.pallas_call(
            back_kernel,
            grid=(steps,),
            in_specs=[
                whole, whole, whole, two(tokens), two(tap_count), two(size), two(EDGE, off), two(tokens),
                three(1, tokens, 0, 1), three(1, tokens, 0, 2),
                three(3, tokens, off), three(3, EDGE, off), three(3, short_len, off),
            ],
            out_specs=[three(3, tokens), three(3, 2 * EDGE), three(3, 2 * EDGE), three(3, EDGE)],
            out_shape=[
                shape3(3, tokens, BF16), shape3(3, 2 * EDGE, BF16), shape3(3, 2 * EDGE, BF16), shape3(3, EDGE, F32),
            ],
            scratch_shapes=[pltpu.VMEM((tokens + EDGE, block), F32)] * 2,
            name=f"back{n}",
            **params(8 * size * tokens * width, 30 * tokens * width),
        )(own, nxt, inv, gf, after, hspec, gain, gq, mixed, mixed, x, edge, short)
        grads.append((gp, tail, head, gs, sums))

    def joined(k, axis):
        return jnp.concatenate([g[k] for g in grads], axis=axis) if chunks > 1 else grads[0][k]

    summed = lax.psum_scatter(totals.astype(BF16), "chan", scatter_dimension=1, tiled=True)
    output = summed.astype(F32).astype(BF16)
    gp, tail, head = joined(0, 2), joined(1, 2), joined(2, 2)
    after = shifted(head[:, :EDGE], "seq", -1)
    grad_proj = pl.pallas_call(
        tail_kernel,
        grid=(channels // block,),
        in_specs=[
            three(3, 2 * EDGE), three(3, EDGE), three(3, short_len), pl.BlockSpec(memory_space=pl.ANY),
        ],
        out_specs=pl.BlockSpec((3, 2 * EDGE, block), lambda c: (0, tokens // (2 * EDGE) - 1, c)),
        out_shape=jax.ShapeDtypeStruct((3, tokens, channels), BF16),
        scratch_shapes=[pltpu.VMEM((3 * EDGE, block), F32)],
        input_output_aliases={3: 0},
        name="tail",
        **params(42 * 16 * channels, 300 * channels),
    )(tail, after, short, gp)
    sums, gs = lax.psum((joined(4, 1), joined(3, 2)), "seq")
    return (
        output,
        grad_proj.transpose(1, 0, 2),
        sums[:tap_count],
        gs[:, :short_len].transpose(1, 0, 2),
        sums[tap_count],
    )


def solution(mesh):
    placed = (
        P("seq", None, "chan"),
        P(None, None, "chan"),
        P(None, "chan"),
        P("chan"),
        P("chan"),
        P("chan", "seq"),
        P("seq", "chan"),
    )
    return jax.shard_map(
        local,
        mesh=mesh,
        in_specs=placed,
        out_specs=(
            P("seq", "chan"),
            P("seq", None, "chan"),
            P(None, "chan"),
            P(None, None, "chan"),
            P("chan"),
        ),
        check_vma=False,
    )
```

time: 1030 us -> 650 us (0.63); the launches traced: 1020 us -> 647 us
  local copies, waits for them, and re-layouts: 439 us -> 28.1 us
  matrix products: 397 us -> 0 us
  waiting for transfers between devices: 8.45 us -> 375 us
  Pallas kernels: 0 us -> 185 us
  other arithmetic: 103 us -> 16.1 us
  blocking collectives: 42.3 us -> 0 us
  starting transfers between devices: 11 us -> 28 us
    conv_general_dilated x6 -> x0, matrix products: 274 us -> none  [depthwise(): lax.conv_general_dilated(signal[None], kernel[:, None, :], (1,), 'VALID',...]
    all_gather x1 -> x4, waiting for transfers between devices: 0.01 us -> 245 us  [local(): panels.append(lax.all_gather(rows, 'seq', axis=1, tiled=True))]
    pallas_call x0 -> x21, Pallas kernels: none -> 185 us  [the longest x4 53.8 us: local(): pl.pallas_call(back_kernel, grid=(steps,), in_specs=[whole, whole, whole,...]
    dot_general x4 -> x0, matrix products: 124 us -> none  [the longest x1 47.3 us: local(): jnp.dot(packed.T, w_out, preferred_element_type=jnp.float32)]
    psum x1, waiting for transfers between devices: 8.4 us -> 129 us  [local(): sums, gs = lax.psum((joined(4, 1), joined(3, 2)), 'seq')]
    convert_element_type x5 -> x0, local copies, waits for them, and re-layouts: 96.6 us -> none  [the longest x4 48.5 us: local(): grad_proj_in = depthwise(padded_mixed, short_taps.reshape(short_len, flat...]
    conv_general_dilated x9 -> x0, local copies, waits for them, and re-layouts: 89.7 us -> none  [depthwise(): lax.conv_general_dilated(signal[None], kernel[:, None, :], (1,), 'VALID',...]
    rev x4 -> x0, local copies, waits for them, and re-layouts: 71.5 us -> none  [the longest x1 32.9 us: local(): grad_long = depthwise(padded_kv, grad_filt_f)[::-1]]
  transfers between devices with their start and end apart: 6 -> 15, of which waited for: 1 -> 6; matrix products, arithmetic and copies ran while one was open for 72% -> 4% of each run, Pallas kernels for 0% -> 26%
where the time goes in v1:
time: 650 us; the launch traced here: 647 us
  waiting for transfers between devices  375 us (58%)
  Pallas kernels  185 us (28%)
  local copies, waits for them, and re-layouts  28.1 us (4%)
  starting transfers between devices  28 us (4%)
  other arithmetic  16.1 us (2%)
  between operations  14.3 us (2%)
    all_gather x4, waiting for transfers between devices, local(): panels.append(lax.all_gather(rows, 'seq', axis=1, tiled=True))  245 us
    psum x1, waiting for transfers between devices, local(): sums, gs = lax.psum((joined(4, 1), joined(3, 2)), 'seq')  129 us
    pallas_call x4, Pallas kernels, local(): pl.pallas_call(back_kernel, grid=(steps,), in_specs=[whole, whole, whole,...  53.8 us
    pallas_call x4, Pallas kernels, local(): pl.pallas_call(grad_kernel, grid=(steps,), in_specs=[whole, whole, pl.Blo...  51.8 us
    pallas_call x4, Pallas kernels, local(): pl.pallas_call(mix_kernel, grid=(steps,), in_specs=[three(3, tokens, off)...  30.4 us
    ppermute x10, starting transfers between devices, shifted(): return lax.ppermute(x, axis, pairs)  27.8 us
    pallas_call x4, Pallas kernels, local(): pl.pallas_call(forward_kernel, grid=(steps,), in_specs=[whole, whole, who...  25.1 us
    pallas_call x4, Pallas kernels, local(): pl.pallas_call(pack_kernel, grid=(steps,), in_specs=[two(EDGE, off), pl.B...  14.4 us
  transfers between devices with their start and end apart: 15, of which 6 were waited for; matrix products, arithmetic and copies ran while one was open for 4% of the time, Pallas kernels for 26%

profile of v1, /device:TPU:0, one launch (start us, length us, event | category | flops | bytes accessed | tf_op | source)
XLA Modules:
  0.0 646.7 jit_solution(5116023340447995185)
XLA Ops:
  10.0 3.6 pack0.1
  13.7 3.6 pack1.1
  17.3 3.6 pack2.1
  21.0 3.6 pack3.1
  25.7 2.4 collective-permute-start
  28.2 1.3 collective-permute-done.edge_ref
  30.2 7.6 %mix0.1 = (f32[3,160,2048]{2,1,0:T(8,128)}, bf16[160,2048]{1,0:T(8,128)(2,1)}) custom-call(bf16[3,160,8192]{2,1,0:T(8,128)(2,1)} %bitcast.7, bf16[3,8,8192]{2,1,0:T(8,128)(2,1)} %copy-done, f32[3,7,8192]{2,1,0:T(8,128)} %bitcast.15), custom_call_target="tpu_custom_call" | custom-call | flops 13762560 | bytes 6553600 | tf_op jit(solution)/shard_map/mix0/pallas_call | solution.py:234
  39.0 7.9 %collective-permute-start.1 = (bf16[128,2048]{1,0:T(8,128)(2,1)S(1)}, bf16[128,2048]{1,0:T(8,128)(2,1)S(1)}, u32[]{:S(2)}, u32[]{:S(2)}) collective-permute-start(bf16[128,2048]{1,0:T(8,128)(2,1)S(1)} %slice.40), channel_id=1, source_target_pairs={{0,1},{1,2},{2,3},{3,4},{4,5},{5,6},{6,7},{7,8},{8,9},{9,10},{10,1... | collective-permute-start | bytes 1572872 | tf_op jit(solution)/shard_map/ppermute | solution.py:21
  46.9 7.6 %mix1.1 = (f32[3,160,2048]{2,1,0:T(8,128)}, bf16[160,2048]{1,0:T(8,128)(2,1)}) custom-call(bf16[3,160,8192]{2,1,0:T(8,128)(2,1)} %bitcast.8, bf16[3,8,8192]{2,1,0:T(8,128)(2,1)} %copy-done, f32[3,7,8192]{2,1,0:T(8,128)} %bitcast.16), custom_call_target="tpu_custom_call" | custom-call | flops 13762560 | bytes 6553600 | tf_op jit(solution)/shard_map/mix1/pallas_call | solution.py:234
  55.6 4.4 collective-permute-start.2
  60.0 7.5 %mix2.1 = (f32[3,160,2048]{2,1,0:T(8,128)}, bf16[160,2048]{1,0:T(8,128)(2,1)}) custom-call(bf16[3,160,8192]{2,1,0:T(8,128)(2,1)} %bitcast.9, bf16[3,8,8192]{2,1,0:T(8,128)(2,1)} %copy-done, f32[3,7,8192]{2,1,0:T(8,128)} %bitcast.17), custom_call_target="tpu_custom_call" | custom-call | flops 13762560 | bytes 6553600 | tf_op jit(solution)/shard_map/mix2/pallas_call | solution.py:234
  67.5 1.1 slice.42
  68.7 2.0 collective-permute-start.3
  70.7 7.5 %mix3.1 = (f32[3,160,2048]{2,1,0:T(8,128)}, bf16[160,2048]{1,0:T(8,128)(2,1)}) custom-call(bf16[3,160,8192]{2,1,0:T(8,128)(2,1)} %bitcast.10, bf16[3,8,8192]{2,1,0:T(8,128)(2,1)} %copy-done, f32[3,7,8192]{2,1,0:T(8,128)} %bitcast.18), custom_call_target="tpu_custom_call" | custom-call | flops 13762560 | bytes 6553600 | tf_op jit(solution)/shard_map/mix3/pallas_call | solution.py:234
  79.3 4.5 collective-permute-start.4
  84.7 6.2 forward0.1
  91.7 6.3 forward1.1
  98.8 6.3 forward2.1
  106.0 6.2 forward3.1
  112.3 6.2 all-gather.5.cloned.1.call-done.panel_ref
  118.4 12.8 %grad0.1 = (f32[160,4096]{1,0:T(8,128)}, bf16[160,2048]{1,0:T(8,128)(2,1)}, bf16[160,2048]{1,0:T(8,128)(2,1)}, f32[136,2048]{1,0:T(8,128)}) custom-call(bf16[288,160]{1,0:T(8,128)(2,1)} %constant.32.clone.own_ref, bf16[160,288]{1,0:T(8,128)(2,1)} %constant.34.clone.inv_ref, bf16[1024,4096]{1,0:T(8,128)(2,1)} %all-gather.5.cloned.1.call-done.panel_ref, ...), custom_call_target="tpu_custom_call" | custom-call | flops 2684354560 | bytes 8388608 | tf_op jit(solution)/shard_map/grad0/pallas_call | solution.py:277
  131.2 1.9 slice.44
  133.1 1.3 collective-permute-start.5
  134.4 81.0 %all-gather.7.cloned.1.call-done.panel_ref = bf16[1024,4096]{1,0:T(8,128)(2,1)} async-done(((bf16[1024,128]{1,0:T(8,128)(2,1)}), bf16[1024,4096]{1,0:T(8,128)(2,1)}) %all-gather.7.cloned.1.call-update) | async-done | bytes 8388624 | tf_op jit(solution)/shard_map/all_gather | solution.py:228
  215.3 13.0 %grad1.1 = (f32[160,4096]{1,0:T(8,128)}, bf16[160,2048]{1,0:T(8,128)(2,1)}, bf16[160,2048]{1,0:T(8,128)(2,1)}, f32[136,2048]{1,0:T(8,128)}) custom-call(bf16[288,160]{1,0:T(8,128)(2,1)} %constant.32.clone.own_ref, bf16[160,288]{1,0:T(8,128)(2,1)} %constant.34.clone.inv_ref, bf16[1024,4096]{1,0:T(8,128)(2,1)} %all-gather.7.cloned.1.call-done.panel_ref, ...), custom_call_target="tpu_custom_call" | custom-call | flops 2684354560 | bytes 8388608 | tf_op jit(solution)/shard_map/grad1/pallas_call | solution.py:277
  228.3 1.9 slice.45
  230.2 1.3 collective-permute-start.6
  231.5 78.9 %all-gather.9.cloned.1.call-done.panel_ref = bf16[1024,4096]{1,0:T(8,128)(2,1)} async-done(((bf16[1024,128]{1,0:T(8,128)(2,1)}), bf16[1024,4096]{1,0:T(8,128)(2,1)}) %all-gather.9.cloned.1.call-update) | async-done | bytes 8388624 | tf_op jit(solution)/shard_map/all_gather | solution.py:228
  310.4 13.0 %grad2.1 = (f32[160,4096]{1,0:T(8,128)}, bf16[160,2048]{1,0:T(8,128)(2,1)}, bf16[160,2048]{1,0:T(8,128)(2,1)}, f32[136,2048]{1,0:T(8,128)}) custom-call(bf16[288,160]{1,0:T(8,128)(2,1)} %constant.32.clone.own_ref, bf16[160,288]{1,0:T(8,128)(2,1)} %constant.34.clone.inv_ref, bf16[1024,4096]{1,0:T(8,128)(2,1)} %all-gather.9.cloned.1.call-done.panel_ref, ...), custom_call_target="tpu_custom_call" | custom-call | flops 2684354560 | bytes 8388608 | tf_op jit(solution)/shard_map/grad2/pallas_call | solution.py:277
  323.4 1.9 slice.46
  325.2 1.3 collective-permute-start.7
  326.5 78.7 %all-gather.11.cloned.1.call-done.panel_ref = bf16[1024,4096]{1,0:T(8,128)(2,1)} async-done(((bf16[1024,128]{1,0:T(8,128)(2,1)}), bf16[1024,4096]{1,0:T(8,128)(2,1)}) %all-gather.11.cloned.1.call-update) | async-done | bytes 8388624 | tf_op jit(solution)/shard_map/all_gather | solution.py:228
  405.2 13.1 %grad3.1 = (f32[160,4096]{1,0:T(8,128)}, bf16[160,2048]{1,0:T(8,128)(2,1)}, bf16[160,2048]{1,0:T(8,128)(2,1)}, f32[136,2048]{1,0:T(8,128)}) custom-call(bf16[288,160]{1,0:T(8,128)(2,1)} %constant.32.clone.own_ref, bf16[160,288]{1,0:T(8,128)(2,1)} %constant.34.clone.inv_ref, bf16[1024,4096]{1,0:T(8,128)(2,1)} %all-gather.11.cloned.1.call-done.panel_ref, ...), custom_call_target="tpu_custom_call" | custom-call | flops 2684354560 | bytes 8388608 | tf_op jit(solution)/shard_map/grad3/pallas_call | solution.py:277
  418.3 1.9 slice.47
  420.2 1.5 collective-permute-start.8
  421.8 3.6 add_convert_fusion
  425.5 2.4 pad_maximum_fusion.1
  427.8 13.4 %back0.1 = (bf16[3,160,2048]{2,1,0:T(8,128)(2,1)}, bf16[3,16,2048]{2,1,0:T(8,128)(2,1)}, bf16[3,16,2048]{2,1,0:T(8,128)(2,1)}, f32[3,8,2048]{2,1,0:T(8,128)}) custom-call(bf16[288,160]{1,0:T(8,128)(2,1)} %constant.32.clone.own_ref, bf16[288,128]{1,0:T(8,128)(2,1)} %constant.33.clone.next_ref, bf16[160,288]{1,0:T(8,128)(2,1)} %constant.34.clone.inv_ref, ...), custom_call_target="tpu_custom_call" | custom-call | flops 754974720 | bytes 9830400 | tf_op jit(solution)/shard_map/back0/pallas_call | solution.py:294
  441.3 13.4 %back1.1 = (bf16[3,160,2048]{2,1,0:T(8,128)(2,1)}, bf16[3,16,2048]{2,1,0:T(8,128)(2,1)}, bf16[3,16,2048]{2,1,0:T(8,128)(2,1)}, f32[3,8,2048]{2,1,0:T(8,128)}) custom-call(bf16[288,160]{1,0:T(8,128)(2,1)} %constant.32.clone.own_ref, bf16[288,128]{1,0:T(8,128)(2,1)} %constant.33.clone.next_ref, bf16[160,288]{1,0:T(8,128)(2,1)} %constant.34.clone.inv_ref, ...), custom_call_target="tpu_custom_call" | custom-call | flops 754974720 | bytes 9830400 | tf_op jit(solution)/shard_map/back1/pallas_call | solution.py:294
  454.7 13.4 %back2.1 = (bf16[3,160,2048]{2,1,0:T(8,128)(2,1)}, bf16[3,16,2048]{2,1,0:T(8,128)(2,1)}, bf16[3,16,2048]{2,1,0:T(8,128)(2,1)}, f32[3,8,2048]{2,1,0:T(8,128)}) custom-call(bf16[288,160]{1,0:T(8,128)(2,1)} %constant.32.clone.own_ref, bf16[288,128]{1,0:T(8,128)(2,1)} %constant.33.clone.next_ref, bf16[160,288]{1,0:T(8,128)(2,1)} %constant.34.clone.inv_ref, ...), custom_call_target="tpu_custom_call" | custom-call | flops 754974720 | bytes 9830400 | tf_op jit(solution)/shard_map/back2/pallas_call | solution.py:294
  468.2 13.5 %back3.1 = (bf16[3,160,2048]{2,1,0:T(8,128)(2,1)}, bf16[3,16,2048]{2,1,0:T(8,128)(2,1)}, bf16[3,16,2048]{2,1,0:T(8,128)(2,1)}, f32[3,8,2048]{2,1,0:T(8,128)}) custom-call(bf16[288,160]{1,0:T(8,128)(2,1)} %constant.32.clone.own_ref, bf16[288,128]{1,0:T(8,128)(2,1)} %constant.33.clone.next_ref, bf16[160,288]{1,0:T(8,128)(2,1)} %constant.34.clone.inv_ref, ...), custom_call_target="tpu_custom_call" | custom-call | flops 754974720 | bytes 9830400 | tf_op jit(solution)/shard_map/back3/pallas_call | solution.py:294
  481.7 1.9 pad_maximum_fusion.3
  484.8 1.3 collective-permute-start.9
  486.2 6.4 pad_maximum_fusion.gp_ref
  494.3 9.5 %tail.1 = bf16[3,160,8192]{2,1,0:T(8,128)(2,1)} custom-call(bf16[3,16,8192]{2,1,0:T(8,128)(2,1)} %pad_maximum_fusion.2.tail_ref, bf16[3,8,8192]{2,1,0:T(8,128)(2,1)} %copy-done.14, f32[3,7,8192]{2,1,0:T(8,128)} %bitcast.23, bf16[3,160,8192]{2,1,0:T(8,128)(2,1)} %pad_maximum_fusion.gp_ref), custom_call_target="tpu_custom_call", output_to_operand_aliasing={{}: (3, {})} | custom-call | flops 5505024 | bytes 2457600 | tf_op jit(solution)/shard_map/tail/pallas_call | solution.py:319
  503.8 129.2 %all-reduce.3.cloned.1.call-done = (f32[136,8192]{1,0:T(8,128)}, f32[3,8,8192]{2,1,0:T(8,128)}) async-done(((f32[136,8192]{1,0:T(8,128)}, f32[3,8,8192]{2,1,0:T(8,128)}), (f32[136,8192]{1,0:T(8,128)}, f32[3,8,8192]{2,1,0:T(8,128)})) %all-reduce.3.cloned.1.call-update) | async-done | bytes 5242896 | tf_op jit(solution)/shard_map/psum | solution.py:332
  633.0 4.7 slice.53
  637.7 1.6 slice.55
  (90 shorter events, 15.3 us)
Async XLA Ops:
  7.2 111.3 %all-gather.5.cloned.1.call-start = ((), (), s32[]{:S(2)}) async-start(), calls=%async_computation | async-start | bytes 8650752 | tf_op jit(solution)/shard_map/all_gather | solution.py:228
  13.6 201.7 %all-gather.7.cloned.1.call-start = ((), (), s32[]{:S(2)}) async-start(), calls=%async_computation.1 | async-start | bytes 8650752 | tf_op jit(solution)/shard_map/all_gather | solution.py:228
  17.3 293.1 %all-gather.9.cloned.1.call-start = ((), (), s32[]{:S(2)}) async-start(), calls=%async_computation.2 | async-start | bytes 8650752 | tf_op jit(solution)/shard_map/all_gather | solution.py:228
  21.0 384.3 %all-gather.11.cloned.1.call-start = ((), (), s32[]{:S(2)}) async-start(), calls=%async_computation.3 | async-start | bytes 8650752 | tf_op jit(solution)/shard_map/all_gather | solution.py:228
  24.6 608.4 %all-reduce.3.cloned.1.call-start = ((), (), s32[]{:S(2)}) async-start(), calls=%async_computation.4 | async-start | bytes 10485760 | tf_op jit(solution)/shard_map/psum | solution.py:332
  25.7 3.7 collective-permute-start
  29.5 0.8 copy-start
  39.0 44.8 %collective-permute-start.1 = (bf16[128,2048]{1,0:T(8,128)(2,1)S(1)}, bf16[128,2048]{1,0:T(8,128)(2,1)S(1)}, u32[]{:S(2)}, u32[]{:S(2)}) collective-permute-start(bf16[128,2048]{1,0:T(8,128)(2,1)S(1)} %slice.40), channel_id=1, source_target_pairs={{0,1},{1,2},{2,3},{3,4},{4,5},{5,6},{6,7},{7,8},{8,9},{9,10},{10,1... | collective-permute-start | bytes 1572872 | tf_op jit(solution)/shard_map/ppermute | solution.py:21
  55.6 35.3 %collective-permute-start.2 = (bf16[128,2048]{1,0:T(8,128)(2,1)S(1)}, bf16[128,2048]{1,0:T(8,128)(2,1)S(1)}, u32[]{:S(2)}, u32[]{:S(2)}) collective-permute-start(bf16[128,2048]{1,0:T(8,128)(2,1)S(1)} %slice.41), channel_id=1, source_target_pairs={{0,1},{1,2},{2,3},{3,4},{4,5},{5,6},{6,7},{7,8},{8,9},{9,10},{10,1... | collective-permute-start | bytes 1572872 | tf_op jit(solution)/shard_map/ppermute | solution.py:21
  68.7 15.1 %copy-start.26 = (f32[8192]{0:T(1024)S(1)}, f32[8192]{0:T(1024)}, u32[]{:S(2)}) copy-start(f32[8192]{0:T(1024)} %param.13) | copy-start | bytes 98308
  68.7 29.4 %collective-permute-start.3 = (bf16[128,2048]{1,0:T(8,128)(2,1)S(1)}, bf16[128,2048]{1,0:T(8,128)(2,1)S(1)}, u32[]{:S(2)}, u32[]{:S(2)}) collective-permute-start(bf16[128,2048]{1,0:T(8,128)(2,1)S(1)} %slice.42), channel_id=1, source_target_pairs={{0,1},{1,2},{2,3},{3,4},{4,5},{5,6},{6,7},{7,8},{8,9},{9,10},{10,1... | collective-permute-start | bytes 1572872 | tf_op jit(solution)/shard_map/ppermute | solution.py:21
  79.3 25.9 %collective-permute-start.4 = (bf16[128,2048]{1,0:T(8,128)(2,1)S(1)}, bf16[128,2048]{1,0:T(8,128)(2,1)S(1)}, u32[]{:S(2)}, u32[]{:S(2)}) collective-permute-start(bf16[128,2048]{1,0:T(8,128)(2,1)S(1)} %slice.43), channel_id=1, source_target_pairs={{0,1},{1,2},{2,3},{3,4},{4,5},{5,6},{6,7},{7,8},{8,9},{9,10},{10,1... | collective-permute-start | bytes 1572872 | tf_op jit(solution)/shard_map/ppermute | solution.py:21
  83.8 0.9 copy-start.13
  90.9 0.8 copy-start.12
  98.1 0.8 copy-start.11
  105.2 0.8 copy-start.10
  133.1 294.7 %collective-permute-start.5 = (bf16[128,2048]{1,0:T(8,128)(2,1)}, bf16[128,2048]{1,0:T(8,128)(2,1)}, u32[]{:S(2)}, u32[]{:S(2)}) collective-permute-start(bf16[128,2048]{1,0:T(8,128)(2,1)} %slice.44), channel_id=1, source_target_pairs={{1,0},{2,1},{3,2},{4,3},{5,4},{6,5},{7,6},{8,7},{9,8},{10,9},{11,1... | collective-permute-start | bytes 1572872 | tf_op jit(solution)/shard_map/ppermute | solution.py:21
  230.2 211.1 %collective-permute-start.6 = (bf16[128,2048]{1,0:T(8,128)(2,1)}, bf16[128,2048]{1,0:T(8,128)(2,1)}, u32[]{:S(2)}, u32[]{:S(2)}) collective-permute-start(bf16[128,2048]{1,0:T(8,128)(2,1)} %slice.45), channel_id=1, source_target_pairs={{1,0},{2,1},{3,2},{4,3},{5,4},{6,5},{7,6},{8,7},{9,8},{10,9},{11,1... | collective-permute-start | bytes 1572872 | tf_op jit(solution)/shard_map/ppermute | solution.py:21
  325.2 129.4 %collective-permute-start.7 = (bf16[128,2048]{1,0:T(8,128)(2,1)}, bf16[128,2048]{1,0:T(8,128)(2,1)}, u32[]{:S(2)}, u32[]{:S(2)}) collective-permute-start(bf16[128,2048]{1,0:T(8,128)(2,1)} %slice.46), channel_id=1, source_target_pairs={{1,0},{2,1},{3,2},{4,3},{5,4},{6,5},{7,6},{8,7},{9,8},{10,9},{11,1... | collective-permute-start | bytes 1572872 | tf_op jit(solution)/shard_map/ppermute | solution.py:21
  405.2 16.5 %copy-start.1 = (f32[160,4096]{1,0:T(8,128)S(1)}, f32[160,4096]{1,0:T(8,128)}, u32[]{:S(2)}) copy-start(f32[160,4096]{1,0:T(8,128)} %get-tuple-element.66) | copy-start | bytes 7864324
  405.2 16.5 %copy-start.2 = (f32[160,4096]{1,0:T(8,128)S(1)}, f32[160,4096]{1,0:T(8,128)}, u32[]{:S(2)}) copy-start(f32[160,4096]{1,0:T(8,128)} %get-tuple-element.72) | copy-start | bytes 7864324
  405.2 16.5 %copy-start.3 = (f32[160,4096]{1,0:T(8,128)S(1)}, f32[160,4096]{1,0:T(8,128)}, u32[]{:S(2)}) copy-start(f32[160,4096]{1,0:T(8,128)} %get-tuple-element.78) | copy-start | bytes 7864324
  420.2 47.9 %collective-permute-start.8 = (bf16[128,2048]{1,0:T(8,128)(2,1)}, bf16[128,2048]{1,0:T(8,128)(2,1)}, u32[]{:S(2)}, u32[]{:S(2)}) collective-permute-start(bf16[128,2048]{1,0:T(8,128)(2,1)} %slice.47), channel_id=1, source_target_pairs={{1,0},{2,1},{3,2},{4,3},{5,4},{6,5},{7,6},{8,7},{9,8},{10,9},{11,1... | collective-permute-start | bytes 1572872 | tf_op jit(solution)/shard_map/ppermute | solution.py:21
  421.8 3.7 copy-start.5
  421.8 3.7 copy-start.6
  421.8 3.7 copy-start.7
  421.8 3.7 copy-start.8
  468.1 13.5 %copy-start.18 = (f32[3,8,2048]{2,1,0:T(8,128)S(1)}, f32[3,8,2048]{2,1,0:T(8,128)}, u32[]{:S(2)}) copy-start(f32[3,8,2048]{2,1,0:T(8,128)} %get-tuple-element.113) | copy-start | bytes 589828
  468.2 13.5 %copy-start.21 = (f32[3,8,2048]{2,1,0:T(8,128)S(1)}, f32[3,8,2048]{2,1,0:T(8,128)}, u32[]{:S(2)}) copy-start(f32[3,8,2048]{2,1,0:T(8,128)} %get-tuple-element.114) | copy-start | bytes 589828
  468.2 13.5 %copy-start.24 = (f32[3,8,2048]{2,1,0:T(8,128)S(1)}, f32[3,8,2048]{2,1,0:T(8,128)}, u32[]{:S(2)}) copy-start(f32[3,8,2048]{2,1,0:T(8,128)} %get-tuple-element.115) | copy-start | bytes 589828
  483.6 0.9 copy-start.16
  483.6 1.0 copy-start.19
  483.6 1.1 copy-start.22
  483.6 1.2 copy-start.25
  483.6 2.5 copy-start.4
  484.8 8.7 %collective-permute-start.9 = (bf16[3,8,8192]{2,1,0:T(8,128)(2,1)S(1)}, bf16[3,8,8192]{2,1,0:T(8,128)(2,1)S(1)}, u32[]{:S(2)}, u32[]{:S(2)}) collective-permute-start(bf16[3,8,8192]{2,1,0:T(8,128)(2,1)S(1)} %pad_maximum_fusion.4), channel_id=1, source_target_pairs={{1,0},{2,1},{3,2},{4,3},{5,4},{6,5},{7,6},{8,7},{9,8},{10,9},{11,1... | collective-permute-start | bytes 1179656 | tf_op jit(solution)/shard_map/ppermute | solution.py:21
  486.1 6.5 %copy-start.15 = (bf16[3,16,2048]{2,1,0:T(8,128)(2,1)S(1)}, bf16[3,16,2048]{2,1,0:T(8,128)(2,1)}, u32[]{:S(2)}) copy-start(bf16[3,16,2048]{2,1,0:T(8,128)(2,1)} %get-tuple-element.88) | copy-start | bytes 589828
  486.1 6.5 copy-start.17
  486.1 6.5 copy-start.20
  486.2 6.5 copy-start.23
  493.6 0.7 copy-start.14
  633.0 6.3 copy-start.9
Sparse Core Ops, SparseCore 0:
  13.7 104.6 all-gather.4
  121.3 94.0 all-gather.6
  218.2 92.1 all-gather.8
  313.1 92.1 all-gather.10
  483.7 149.2 all-reduce.2
